TPU v7x, 256 devices: a whole 4x4x8 slice. The times are simulated.
256 devices in a mesh: row: 32 (over y, z), col: 8 (over x, core).
Axes of the slice: x: 4, y: 4, z: 8, core: 2. Of those that a mesh axis runs over, the one named last changes fastest.
Arguments:
- ancestor_inverse: float32 [12288, 12288], P('row', 'col'), may hold values from -5 to 320, as said below
- panel_one: float32 [12288, 256], P(('row', 'col')), may hold values from -0.015625 to 0.015625
- struct_one: int32 [10752], replicated, may hold values from 0 to 12287, as said below
- lower_one: float32 [256, 256], replicated, may hold values from -1 to 2, as said below
- panel_two: float32 [12288, 256], P(('row', 'col')), may hold values from -0.015625 to 0.015625
- struct_two: int32 [9216], replicated, may hold values from 0 to 12287, as said below
- panel_above: float32 [256, 256], replicated, may hold values from -0.375 to 0.375
- lower_two: float32 [256, 256], replicated, may hold values from -1 to 2, as said below
- tile_owner: int32 [1536, 1], P(('col', 'row')), may hold values from 0 to 7; in each aligned block of 6 rows (0 to 5, 6 to 11, ...) at most 2 rows name the same one
Outputs:
- inverse_one: float32 [12288, 256], P(('col', 'row'))
- diag_one: float32 [256, 256], replicated
- cross_two: float32 [256, 256], replicated
- diag_two: float32 [256, 256], replicated
- delivered: float32 [4096, 8, 256], P(('row', 'col'))
Inputs may be any that keep to these rules, and one draw needn't show every extreme that they name: ancestor_inverse is exactly symmetric and positive definite. `struct_one`: 10752 distinct row numbers of the ancestor block. `struct_two`: 9216 distinct entries of struct_one. `lower_one`: lower triangular with a positive diagonal. `lower_two`: lower triangular with a positive diagonal. `tile_owner`: within each aligned block of 6 entries (the tiles of one device) no value appears more than 2 times; in some block a value appears exactly 2 times.
All inputs are finite; a program needn't handle non-finite values.
Results may differ from a plain program's by a relative error of at most 0.00007.
Values sent between devices are 32-bit elements; how exact they have to be, the bound alone decides.
No kernel may reach another device: no remote copies, remote signals or barrier semaphores. Data moves between devices by JAX's collectives and lax.ppermute only.
A program may use at most 64 MiB of HBM per device.

v0:
```python
import jax
import jax.numpy as jnp
from jax import lax
from jax.sharding import Mesh
from jax.sharding import PartitionSpec as P

CAP = 2
COL = ("col_0", "col_1")
ROW = ("row_0", "row_1")
ROW_COL = ROW + COL
COL_ROW = COL + ROW
N_ROW = 32
N_COL = 8
N_Y, N_Z = (4, 8)


def row_mask(listed, start, count):
    rows = start + jnp.arange(count, dtype=jnp.int32)
    hit = listed[None, :] == rows[:, None]
    return jnp.max(jnp.where(hit, 1.0, 0.0), axis=1, keepdims=True)


def dot(left, right, dims=((1,), (0,)), precision=lax.Precision.HIGHEST):
    return lax.dot_general(
        left, right, (dims, ((), ())), precision=precision, preferred_element_type=jnp.float32
    )


def sum_at_owner(value, axis):
    count = lax.axis_size(axis)
    parts = value.reshape(count, value.shape[0] // count, *value.shape[1:])
    return jnp.sum(lax.all_to_all(parts, axis, 0, 0, tiled=True), axis=0)


def copies_of(value, axis):
    copies = jnp.broadcast_to(value[None], (lax.axis_size(axis), *value.shape))
    return lax.all_to_all(copies, axis, 0, 0, tiled=True)


def total(value):
    own = sum_at_owner(sum_at_owner(value, COL), ROW)
    over_row = copies_of(own, ROW).reshape(-1, value.shape[1])
    return copies_of(over_row, COL).reshape(value.shape)


def gather_moves():
    pairs = []
    for block in range(N_ROW * N_COL):
        column, place = divmod(block, N_ROW)
        z, y = divmod(place, N_Y)
        pairs.append((block, (y * N_Z + z) * N_COL + column))
    return pairs


def result_moves():
    pairs = []
    for block in range(N_ROW * N_COL):
        column, row = divmod(block, N_ROW)
        pairs.append((block, row * N_COL + column))
    return pairs


def deliver(values, tile_owner):
    tile_count = tile_owner.shape[0]
    tile_rows = values.shape[0] // tile_count
    all_tiles = values.reshape(tile_count, tile_rows, values.shape[1])
    owner = tile_owner[:, 0]
    order = jnp.arange(tile_count)
    same = (owner[:, None] == owner[None, :]) & (order[None, :] < order[:, None])
    rank = jnp.sum(same.astype(jnp.int32), axis=1)
    select = (
        (owner[None, None, :] == jnp.arange(N_COL)[:, None, None])
        & (rank[None, None, :] == jnp.arange(CAP)[None, :, None])
    ).astype(jnp.float32)
    outgoing = jnp.einsum("cks,srb->ckrb", select, all_tiles, precision=lax.Precision.HIGHEST)
    incoming = lax.all_to_all(outgoing, COL, split_axis=0, concat_axis=0, tiled=True)
    return incoming.reshape(N_COL * CAP, tile_rows, values.shape[1])


def local(
    ancestor_inverse,
    panel_one,
    struct_one,
    lower_one,
    panel_two,
    struct_two,
    panel_above,
    lower_two,
    tile_owner,
):
    row_index = lax.axis_index(ROW)
    col_index = lax.axis_index(COL)
    local_rows, width = panel_one.shape
    start = (row_index * N_COL + col_index) * local_rows
    mask_one = row_mask(struct_one, start, local_rows)
    mask_two = row_mask(struct_two, start, local_rows)
    panels = jnp.concatenate([panel_one * mask_one, panel_two * mask_two], axis=1)
    placed = lax.ppermute(panels, ROW_COL, gather_moves())
    column_panels = lax.all_gather(placed, "row_0", axis=0, tiled=True)
    column_panels = lax.all_gather(column_panels, "row_1", axis=0, tiled=True)
    row_panels = lax.all_gather(panels, COL, axis=0, tiled=True)
    product = dot(ancestor_inverse, column_panels, precision=lax.Precision.HIGH)
    from_one = dot(row_panels[:, :width], product, ((0,), (0,)), lax.Precision.HIGH)
    from_two = dot(row_panels[:, width:], product[:, width:], ((0,), (0,)), lax.Precision.HIGH)
    partial = jnp.concatenate([from_one[:, :width], from_one[:, width:], from_two], axis=0)
    grams = total(partial)
    w_one, w_cross, w_two = (grams[:width], grams[width : 2 * width], grams[2 * width :])
    diag_one = dot(lower_one, lower_one, ((0,), (0,))) + w_one
    cross_two = w_cross - dot(diag_one, panel_above)
    diag_two = (
        dot(lower_two, lower_two, ((0,), (0,)))
        + w_two
        - dot(w_cross, panel_above, ((0,), (0,)))
        - dot(panel_above, cross_two, ((0,), (0,)))
    )
    rows = sum_at_owner(product, COL)
    inverse_one = -rows[:, :width] * mask_one
    inverse_two = -(rows[:, width:] + dot(inverse_one, panel_above)) * mask_two
    inverses = lax.ppermute(
        jnp.concatenate([inverse_one, inverse_two], axis=1), ROW_COL, result_moves()
    )
    inverse_one, inverse_two = (inverses[:, :width], inverses[:, width:])
    delivered = deliver(inverse_two, tile_owner)
    return (inverse_one, diag_one, cross_two, diag_two, delivered)


def solution(mesh):
    finer = Mesh(mesh.devices.reshape(4, 8, 4, 2), ("row_0", "row_1", "col_0", "col_1"))
    return jax.shard_map(
        local,
        mesh=finer,
        in_specs=(
            P(ROW, COL),
            P(ROW_COL, None),
            P(),
            P(),
            P(ROW_COL, None),
            P(),
            P(),
            P(),
            P(COL_ROW, None),
        ),
        out_specs=(P(COL_ROW, None), P(), P(), P(), P(ROW_COL, None, None)),
        check_vma=False,
    )
```

profile of v0, /device:TPU:1, one launch (start us, length us, event | category | flops | bytes accessed | tf_op | source)
XLA Modules:
  0.0 209.6 jit_solution(13605550530463847932)
XLA Ops:
  7.2 0.0 copy-start
  7.2 0.0 all-gather.2.cloned.1.call-start
  7.2 1.3 select_reduce_fusion
  8.6 1.1 select_reduce_fusion.1
  9.7 0.9 broadcast_multiply_fusion
  10.6 4.6 %collective-permute-start = (f32[48,512]{1,0:T(8,128)S(1)}, f32[48,512]{1,0:T(8,128)S(1)}, u32[]{:S(2)}, u32[]{:S(2)}) collective-permute-start(f32[48,512]{1,0:T(8,128)S(1)} %pad_maximum_fusion.1), channel_id=1, source_target_pairs={{0,0},{1,64},{2,128},{3,192},{4,8},{5,72},{6,136},{7,200},{8,16},{... | collective-permute-start | bytes 294920 | tf_op jit(solution)/shard_map/ppermute | solution.py:98
  15.2 8.1 %collective-permute-done = f32[48,512]{1,0:T(8,128)S(1)} collective-permute-done((f32[48,512]{1,0:T(8,128)S(1)}, f32[48,512]{1,0:T(8,128)S(1)}, u32[]{:S(2)}, u32[]{:S(2)}) %collective-permute-start) | collective-permute-done | bytes 98336 | tf_op jit(solution)/shard_map/ppermute | solution.py:98
  23.3 12.5 %all_gather.9 = f32[192,512]{1,0:T(8,128)} all-gather(f32[48,512]{1,0:T(8,128)S(1)} %collective-permute-done), channel_id=1, replica_groups=mesh['row_0'=4,'row_1'=8,'col_0'=4,'col_1'=2] {'row_0'}, dimensions={0}, use_global_device_ids=true | all-gather | bytes 491520 | tf_op jit(solution)/shard_map/all_gather | solution.py:99
  35.8 0.0 all-gather.2.cloned.1.call-update
  35.8 0.9 convert_reduce_fusion
  36.7 0.7 iota_compare_fusion.1
  37.4 17.0 %all_gather.11 = f32[384,512]{1,0:T(8,128)} all-gather(f32[48,512]{1,0:T(8,128)S(1)} %pad_maximum_fusion.1), channel_id=1, replica_groups=mesh['row_0'=4,'row_1'=8,'col_0'=4,'col_1'=2] {'col_0','col_1'}, dimensions={0}, use_global_device_ids=true | all-gather | bytes 884736 | tf_op jit(solution)/shard_map/all_gather | solution.py:101
  54.4 34.5 %all-gather.2.cloned.1.call-done = f32[1536,512]{1,0:T(8,128)} async-done(((f32[192,512]{1,0:T(8,128)}), f32[1536,512]{1,0:T(8,128)}) %all-gather.2.cloned.1.call-update) | async-done | bytes 3145744 | tf_op jit(solution)/shard_map/all_gather | solution.py:100
  88.8 4.8 %fusion.19 = f32[512,384]{0,1:T(8,128)} fusion(f32[1536,512]{1,0:T(8,128)} %all-gather.2.cloned.1.call-done, f32[384,1536]{1,0:T(8,128)S(1)} %copy-done), kind=kOutput, calls=%fused_computation.39 | convolution fusion | flops 1811939328 | bytes 6291456 | tf_op jit(solution)/shard_map/dot_general | solution.py:24
  93.7 5.2 %all-to-all-start = ((f32[8,48,512]{2,1,0:T(8,128)}), f32[8,48,512]{2,1,0:T(8,128)S(1)}, u32[]{:S(2)}, u32[]{:S(2)}) async-start(f32[8,48,512]{2,1,0:T(8,128)} %bitcast.1), calls=%async_computation | async-start | bytes 1572864 | tf_op jit(solution)/shard_map/all_to_all | solution.py:32
  98.9 1.9 fusion.6
  100.9 1.5 fusion.3
  102.4 0.9 pad_maximum_fusion
  103.3 7.8 %all-to-all-done = f32[8,48,512]{2,1,0:T(8,128)S(1)} async-done(((f32[8,48,512]{2,1,0:T(8,128)}), f32[8,48,512]{2,1,0:T(8,128)S(1)}, u32[]{:S(2)}, u32[]{:S(2)}) %all-to-all-start) | async-done | bytes 786464 | tf_op jit(solution)/shard_map/all_to_all | solution.py:32
  111.1 5.0 %all-to-all-start.1 = ((f32[8,96,256]{2,1,0:T(8,128)}), f32[8,96,256]{2,1,0:T(8,128)}, u32[]{:S(2)}, u32[]{:S(2)}) async-start(f32[8,96,256]{2,1,0:T(8,128)} %bitcast.2), calls=%async_computation.1 | async-start | bytes 1572864 | tf_op jit(solution)/shard_map/all_to_all | solution.py:32
  116.1 0.1 reduce_sum.36
  116.2 0.1 fusion.12
  116.3 0.2 fusion.2
  116.5 2.9 %collective-permute-start.1 = (f32[48,512]{1,0:T(8,128)S(1)}, f32[48,512]{1,0:T(8,128)S(1)}, u32[]{:S(2)}, u32[]{:S(2)}) collective-permute-start(f32[48,512]{1,0:T(8,128)S(1)} %pad_maximum_fusion.2), channel_id=1, source_target_pairs={{0,0},{1,8},{2,16},{3,24},{4,32},{5,40},{6,48},{7,56},{8,64},{9,72... | collective-permute-start | bytes 294920 | tf_op jit(solution)/shard_map/ppermute | solution.py:119
  119.4 9.1 %all-to-all-done.1 = f32[8,96,256]{2,1,0:T(8,128)} async-done(((f32[8,96,256]{2,1,0:T(8,128)}), f32[8,96,256]{2,1,0:T(8,128)}, u32[]{:S(2)}, u32[]{:S(2)}) %all-to-all-start.1) | async-done | bytes 786464 | tf_op jit(solution)/shard_map/all_to_all | solution.py:32
  128.5 1.2 reduce_sum.37
  129.7 0.7 reshape.90
  130.4 14.0 %all-to-all-start.2 = ((f32[32,3,256]{2,1,0:T(4,128)}), f32[32,3,256]{2,1,0:T(4,128)S(1)}, u32[]{:S(2)}, u32[]{:S(2)}) async-start(f32[32,3,256]{2,1,0:T(4,128)} %reshape.90), calls=%async_computation.2 | async-start | bytes 262144 | tf_op jit(solution)/shard_map/all_to_all | solution.py:32
  144.4 0.6 slice_bitcast_fusion
  145.1 8.5 %all-to-all-done.2 = f32[32,3,256]{2,1,0:T(4,128)S(1)} async-done(((f32[32,3,256]{2,1,0:T(4,128)}), f32[32,3,256]{2,1,0:T(4,128)S(1)}, u32[]{:S(2)}, u32[]{:S(2)}) %all-to-all-start.2) | async-done | bytes 98336 | tf_op jit(solution)/shard_map/all_to_all | solution.py:32
  153.6 0.7 broadcast_in_dim.44
  154.3 3.9 %all-to-all-start.3 = ((f32[32,3,256]{2,1,0:T(4,128)}), f32[32,3,256]{2,1,0:T(4,128)S(1)}, u32[]{:S(2)}, u32[]{:S(2)}) async-start(f32[32,3,256]{2,1,0:T(4,128)} %broadcast_in_dim.44), calls=%async_computation.3 | async-start | bytes 262144 | tf_op jit(solution)/shard_map/all_to_all | solution.py:37
  158.2 0.2 fusion.9
  158.4 0.7 copy.24
  159.1 8.3 %all-to-all-done.3 = f32[32,3,256]{2,1,0:T(4,128)S(1)} async-done(((f32[32,3,256]{2,1,0:T(4,128)}), f32[32,3,256]{2,1,0:T(4,128)S(1)}, u32[]{:S(2)}, u32[]{:S(2)}) %all-to-all-start.3) | async-done | bytes 98336 | tf_op jit(solution)/shard_map/all_to_all | solution.py:37
  167.3 7.3 %all-to-all-start.5 = ((f32[8,2,8,256]{3,2,1,0:T(8,128)}), f32[8,2,8,256]{3,2,1,0:T(8,128)S(1)}, u32[]{:S(2)}, u32[]{:S(2)}) async-start(f32[8,2,8,256]{3,2,1,0:T(8,128)} %copy.24), calls=%async_computation.5 | async-start | bytes 262144 | tf_op jit(solution)/shard_map/all_to_all | solution.py:76
  174.7 5.2 %all-to-all-done.5 = f32[8,2,8,256]{3,2,1,0:T(8,128)S(1)} async-done(((f32[8,2,8,256]{3,2,1,0:T(8,128)}), f32[8,2,8,256]{3,2,1,0:T(8,128)S(1)}, u32[]{:S(2)}, u32[]{:S(2)}) %all-to-all-start.5) | async-done | bytes 131104 | tf_op jit(solution)/shard_map/all_to_all | solution.py:76
  179.9 1.0 broadcast_in_dim.46
  180.9 4.3 %all-to-all-start.4 = ((f32[8,96,256]{2,1,0:T(8,128)}), f32[8,96,256]{2,1,0:T(8,128)S(1)}, u32[]{:S(2)}, u32[]{:S(2)}) async-start(f32[8,96,256]{2,1,0:T(8,128)} %broadcast_in_dim.46), calls=%async_computation.4 | async-start | bytes 1572864 | tf_op jit(solution)/shard_map/all_to_all | solution.py:37
  185.2 12.3 %all-to-all-done.4 = f32[8,96,256]{2,1,0:T(8,128)S(1)} async-done(((f32[8,96,256]{2,1,0:T(8,128)}), f32[8,96,256]{2,1,0:T(8,128)S(1)}, u32[]{:S(2)}, u32[]{:S(2)}) %all-to-all-start.4) | async-done | bytes 786464 | tf_op jit(solution)/shard_map/all_to_all | solution.py:37
  197.5 1.7 convolution_add_fusion
  199.2 0.6 convolution_subtract_fusion
  199.8 0.6 convolution_add_fusion.1
  200.4 0.0 copy-start.4
  200.4 0.4 convolution_subtract_fusion.1
  200.8 0.0 copy-start.5
  200.8 1.3 fusion
  202.1 0.7 copy.32
  (17 shorter events, 0.2 us)
Async XLA Ops:
  7.2 81.7 %copy-start = (f32[384,1536]{1,0:T(8,128)S(1)}, f32[384,1536]{1,0:T(8,128)}, u32[]{:S(2)}) copy-start(f32[384,1536]{1,0:T(8,128)} %param.9) | copy-start | bytes 7077892
  7.2 81.7 %all-gather.2.cloned.1.call-start = ((), (), s32[]{:S(2)}) async-start(), calls=%async_computation.6 | async-start | bytes 3538944 | tf_op jit(solution)/shard_map/all_gather | solution.py:100
  10.6 12.7 %collective-permute-start = (f32[48,512]{1,0:T(8,128)S(1)}, f32[48,512]{1,0:T(8,128)S(1)}, u32[]{:S(2)}, u32[]{:S(2)}) collective-permute-start(f32[48,512]{1,0:T(8,128)S(1)} %pad_maximum_fusion.1), channel_id=1, source_target_pairs={{0,0},{1,64},{2,128},{3,192},{4,8},{5,72},{6,136},{7,200},{8,16},{... | collective-permute-start | bytes 294920 | tf_op jit(solution)/shard_map/ppermute | solution.py:98
  93.7 17.4 %all-to-all-start = ((f32[8,48,512]{2,1,0:T(8,128)}), f32[8,48,512]{2,1,0:T(8,128)S(1)}, u32[]{:S(2)}, u32[]{:S(2)}) async-start(f32[8,48,512]{2,1,0:T(8,128)} %bitcast.1), calls=%async_computation | async-start | bytes 1572864 | tf_op jit(solution)/shard_map/all_to_all | solution.py:32
  98.9 2.0 copy-start.2
  102.4 13.9 %copy-start.1 = (f32[256,256]{1,0:T(8,128)S(1)}, f32[256,256]{1,0:T(8,128)}, u32[]{:S(2)}) copy-start(f32[256,256]{1,0:T(8,128)} %param.15) | copy-start | bytes 786436
  111.1 17.4 %all-to-all-start.1 = ((f32[8,96,256]{2,1,0:T(8,128)}), f32[8,96,256]{2,1,0:T(8,128)}, u32[]{:S(2)}, u32[]{:S(2)}) async-start(f32[8,96,256]{2,1,0:T(8,128)} %bitcast.2), calls=%async_computation.1 | async-start | bytes 1572864 | tf_op jit(solution)/shard_map/all_to_all | solution.py:32
  116.5 27.9 %collective-permute-start.1 = (f32[48,512]{1,0:T(8,128)S(1)}, f32[48,512]{1,0:T(8,128)S(1)}, u32[]{:S(2)}, u32[]{:S(2)}) collective-permute-start(f32[48,512]{1,0:T(8,128)S(1)} %pad_maximum_fusion.2), channel_id=1, source_target_pairs={{0,0},{1,8},{2,16},{3,24},{4,32},{5,40},{6,48},{7,56},{8,64},{9,72... | collective-permute-start | bytes 294920 | tf_op jit(solution)/shard_map/ppermute | solution.py:119
  130.4 23.2 %all-to-all-start.2 = ((f32[32,3,256]{2,1,0:T(4,128)}), f32[32,3,256]{2,1,0:T(4,128)S(1)}, u32[]{:S(2)}, u32[]{:S(2)}) async-start(f32[32,3,256]{2,1,0:T(4,128)} %reshape.90), calls=%async_computation.2 | async-start | bytes 262144 | tf_op jit(solution)/shard_map/all_to_all | solution.py:32
  154.3 13.0 %all-to-all-start.3 = ((f32[32,3,256]{2,1,0:T(4,128)}), f32[32,3,256]{2,1,0:T(4,128)S(1)}, u32[]{:S(2)}, u32[]{:S(2)}) async-start(f32[32,3,256]{2,1,0:T(4,128)} %broadcast_in_dim.44), calls=%async_computation.3 | async-start | bytes 262144 | tf_op jit(solution)/shard_map/all_to_all | solution.py:37
  167.3 12.6 %all-to-all-start.5 = ((f32[8,2,8,256]{3,2,1,0:T(8,128)}), f32[8,2,8,256]{3,2,1,0:T(8,128)S(1)}, u32[]{:S(2)}, u32[]{:S(2)}) async-start(f32[8,2,8,256]{3,2,1,0:T(8,128)} %copy.24), calls=%async_computation.5 | async-start | bytes 262144 | tf_op jit(solution)/shard_map/all_to_all | solution.py:76
  180.9 16.6 %all-to-all-start.4 = ((f32[8,96,256]{2,1,0:T(8,128)}), f32[8,96,256]{2,1,0:T(8,128)S(1)}, u32[]{:S(2)}, u32[]{:S(2)}) async-start(f32[8,96,256]{2,1,0:T(8,128)} %broadcast_in_dim.46), calls=%async_computation.4 | async-start | bytes 1572864 | tf_op jit(solution)/shard_map/all_to_all | solution.py:37
  197.5 2.3 %copy-start.3 = (f32[256,256]{1,0:T(8,128)S(1)}, f32[256,256]{1,0:T(8,128)}, u32[]{:S(2)}) copy-start(f32[256,256]{1,0:T(8,128)} %param.12) | copy-start | bytes 786436
  200.4 2.4 %copy-start.4 = (f32[256,256]{1,0:T(8,128)}, f32[256,256]{1,0:T(8,128)S(1)}, u32[]{:S(2)}) copy-start(f32[256,256]{1,0:T(8,128)S(1)} %convolution_add_fusion.1) | copy-start | bytes 786436
  200.8 2.0 copy-start.5
Sparse Core Ops, SparseCore 0:
  35.9 52.8 all-gather.1
where the time goes:
time: 211 us; the launch traced here: 210 us
  waiting for transfers between devices  93.9 us (45%)
  starting transfers between devices  47.1 us (22%)
  blocking collectives  29.4 us (14%)
  between operations  14.3 us (7%)
  matrix products  13.3 us (6%)
  other arithmetic  7.24 us (3%)
  local copies, waits for them, and re-layouts  4.43 us (2%)
    all_gather x1, waiting for transfers between devices, local(): column_panels = lax.all_gather(column_panels, 'row_1', axis=0, tiled=True)  34.5 us
    all_to_all x3, waiting for transfers between devices, sum_at_owner(): return jnp.sum(lax.all_to_all(parts, axis, 0, 0, tiled=True), axis=0)  25.5 us
    all_to_all x3, starting transfers between devices, sum_at_owner(): return jnp.sum(lax.all_to_all(parts, axis, 0, 0, tiled=True), axis=0)  24.1 us
    all_to_all x2, waiting for transfers between devices, copies_of(): return lax.all_to_all(copies, axis, 0, 0, tiled=True)  20.6 us
    all_gather x1, blocking collectives, local(): row_panels = lax.all_gather(panels, COL, axis=0, tiled=True)  17 us
    dot_general x9, matrix products, dot(): lax.dot_general(left, right, (dims, ((), ())), precision=precision, prefe...  13.1 us
    all_gather x1, blocking collectives, local(): column_panels = lax.all_gather(placed, 'row_0', axis=0, tiled=True)  12.5 us
    all_to_all x2, starting transfers between devices, copies_of(): return lax.all_to_all(copies, axis, 0, 0, tiled=True)  8.17 us
  transfers between devices with their start and end apart: 9, of which 8 were waited for; matrix products, arithmetic and copies ran while one was open for 5% of the time, Pallas kernels for 0%

commit v1 on v0

--- a/solution.py
+++ b/solution.py
@@ -97,7 +97,9 @@
     panels = jnp.concatenate([panel_one * mask_one, panel_two * mask_two], axis=1)
     placed = lax.ppermute(panels, ROW_COL, gather_moves())
     column_panels = lax.all_gather(placed, "row_0", axis=0, tiled=True)
-    column_panels = lax.all_gather(column_panels, "row_1", axis=0, tiled=True)
+    column_panels = jnp.concatenate(
+        lax.all_to_all(jnp.stack([column_panels] * lax.axis_size("row_1")), "row_1", 0, 0), axis=0
+    )
     row_panels = lax.all_gather(panels, COL, axis=0, tiled=True)
     product = dot(ancestor_inverse, column_panels, precision=lax.Precision.HIGH)
     from_one = dot(row_panels[:, :width], product, ((0,), (0,)), lax.Precision.HIGH)

time: 211 us -> 226 us (1.071)
  between operations: 14.3 us -> 0.87 us
  waiting for transfers between devices: 93.9 us -> 107 us
  starting transfers between devices: 47.1 us -> 57.2 us
  blocking collectives: 29.4 us -> 33.5 us
    all_to_all x0 -> x1, waiting for transfers between devices: none -> 47.5 us  [local(): lax.all_to_all(jnp.stack([column_panels] * lax.axis_size('row_1')), 'row_...]
    all_gather x1 -> x0, waiting for transfers between devices: 34.5 us -> none  [local(): column_panels = lax.all_gather(column_panels, 'row_1', axis=0, tiled=True)]
    all_to_all x0 -> x1, starting transfers between devices: none -> 9.06 us  [local(): lax.all_to_all(jnp.stack([column_panels] * lax.axis_size('row_1')), 'row_...]
    all_gather x1, blocking collectives: 17 us -> 21.7 us  [local(): row_panels = lax.all_gather(panels, COL, axis=0, tiled=True)]
  transfers between devices with their start and end apart: 9 -> 9, of which waited for: 8 -> 8; matrix products, arithmetic and copies ran while one was open for 5% -> 4% of each run, Pallas kernels for 0% -> 0%
where the time goes in v1:
time: 226 us; the launch traced here: 225 us
  waiting for transfers between devices  107 us (47%)
  starting transfers between devices  57.2 us (25%)
  blocking collectives  33.5 us (15%)
  matrix products  13.3 us (6%)
  local copies, waits for them, and re-layouts  6.53 us (3%)
  other arithmetic  5.86 us (3%)
    all_to_all x1, waiting for transfers between devices, local(): lax.all_to_all(jnp.stack([column_panels] * lax.axis_size('row_1')), 'row_...  47.5 us
    all_to_all x3, waiting for transfers between devices, sum_at_owner(): return jnp.sum(lax.all_to_all(parts, axis, 0, 0, tiled=True), axis=0)  26.1 us
    all_to_all x3, starting transfers between devices, sum_at_owner(): return jnp.sum(lax.all_to_all(parts, axis, 0, 0, tiled=True), axis=0)  25.8 us
    all_gather x1, blocking collectives, local(): row_panels = lax.all_gather(panels, COL, axis=0, tiled=True)  21.7 us
    all_to_all x2, waiting for transfers between devices, copies_of(): return lax.all_to_all(copies, axis, 0, 0, tiled=True)  20.6 us
    dot_general x9, matrix products, dot(): lax.dot_general(left, right, (dims, ((), ())), precision=precision, prefe...  13.1 us
    all_gather x1, blocking collectives, local(): column_panels = lax.all_gather(placed, 'row_0', axis=0, tiled=True)  11.7 us
    all_to_all x1, starting transfers between devices, local(): lax.all_to_all(jnp.stack([column_panels] * lax.axis_size('row_1')), 'row_...  9.06 us
  transfers between devices with their start and end apart: 9, of which 8 were waited for; matrix products, arithmetic and copies ran while one was open for 4% of the time, Pallas kernels for 0%

profile of v1, /device:TPU:1, one launch (start us, length us, event | category | flops | bytes accessed | tf_op | source)
XLA Modules:
  0.0 224.7 jit_solution(9630679193038962177)
XLA Ops:
  0.6 0.0 copy-start
  0.7 1.3 select_reduce_fusion
  2.0 1.1 select_reduce_fusion.1
  3.1 0.9 broadcast_multiply_fusion
  4.0 4.6 %collective-permute-start = (f32[48,512]{1,0:T(8,128)S(1)}, f32[48,512]{1,0:T(8,128)S(1)}, u32[]{:S(2)}, u32[]{:S(2)}) collective-permute-start(f32[48,512]{1,0:T(8,128)S(1)} %pad_maximum_fusion.1), channel_id=1, source_target_pairs={{0,0},{1,64},{2,128},{3,192},{4,8},{5,72},{6,136},{7,200},{8,16},{... | collective-permute-start | bytes 294920 | tf_op jit(solution)/shard_map/ppermute | solution.py:98
  8.6 8.1 %collective-permute-done = f32[48,512]{1,0:T(8,128)S(1)} collective-permute-done((f32[48,512]{1,0:T(8,128)S(1)}, f32[48,512]{1,0:T(8,128)S(1)}, u32[]{:S(2)}, u32[]{:S(2)}) %collective-permute-start) | collective-permute-done | bytes 98336 | tf_op jit(solution)/shard_map/ppermute | solution.py:98
  16.7 11.7 %all_gather.6 = f32[192,512]{1,0:T(8,128)S(1)} all-gather(f32[48,512]{1,0:T(8,128)S(1)} %collective-permute-done), channel_id=1, replica_groups=mesh['row_0'=4,'row_1'=8,'col_0'=4,'col_1'=2] {'row_0'}, dimensions={0}, use_global_device_ids=true | all-gather | bytes 491520 | tf_op jit(solution)/shard_map/all_gather | solution.py:99
  28.4 2.1 stack.2
  30.5 9.1 %all-to-all-start = ((f32[8,192,512]{2,1,0:T(8,128)}), f32[8,192,512]{2,1,0:T(8,128)}, u32[]{:S(2)}, u32[]{:S(2)}) async-start(f32[8,192,512]{2,1,0:T(8,128)} %stack.2), calls=%async_computation | async-start | bytes 6291456 | tf_op jit(solution)/shard_map/all_to_all | solution.py:101
  39.6 0.2 convert_reduce_fusion
  39.8 21.7 %all_gather.7 = f32[384,512]{1,0:T(8,128)} all-gather(f32[48,512]{1,0:T(8,128)S(1)} %pad_maximum_fusion.1), channel_id=1, replica_groups=mesh['row_0'=4,'row_1'=8,'col_0'=4,'col_1'=2] {'col_0','col_1'}, dimensions={0}, use_global_device_ids=true | all-gather | bytes 884736 | tf_op jit(solution)/shard_map/all_gather | solution.py:103
  61.5 47.5 %all-to-all-done = f32[8,192,512]{2,1,0:T(8,128)} async-done(((f32[8,192,512]{2,1,0:T(8,128)}), f32[8,192,512]{2,1,0:T(8,128)}, u32[]{:S(2)}, u32[]{:S(2)}) %all-to-all-start) | async-done | bytes 3145760 | tf_op jit(solution)/shard_map/all_to_all | solution.py:101
  109.0 4.8 %fusion.19 = f32[512,384]{0,1:T(8,128)} fusion(f32[1536,512]{1,0:T(8,128)} %bitcast, f32[384,1536]{1,0:T(8,128)S(1)} %copy-done), kind=kOutput, calls=%fused_computation.39 | convolution fusion | flops 1811939328 | bytes 6291456 | tf_op jit(solution)/shard_map/dot_general | solution.py:24
  113.8 11.5 %all-to-all-start.1 = ((f32[8,48,512]{2,1,0:T(8,128)}), f32[8,48,512]{2,1,0:T(8,128)S(1)}, u32[]{:S(2)}, u32[]{:S(2)}) async-start(f32[8,48,512]{2,1,0:T(8,128)} %bitcast.2), calls=%async_computation.1 | async-start | bytes 1572864 | tf_op jit(solution)/shard_map/all_to_all | solution.py:32
  125.4 1.9 fusion.6
  127.4 1.5 fusion.3
  128.9 0.0 copy-start.1
  128.9 0.9 pad_maximum_fusion
  129.8 7.8 %all-to-all-done.1 = f32[8,48,512]{2,1,0:T(8,128)S(1)} async-done(((f32[8,48,512]{2,1,0:T(8,128)}), f32[8,48,512]{2,1,0:T(8,128)S(1)}, u32[]{:S(2)}, u32[]{:S(2)}) %all-to-all-start.1) | async-done | bytes 786464 | tf_op jit(solution)/shard_map/all_to_all | solution.py:32
  137.6 5.0 %all-to-all-start.2 = ((f32[8,96,256]{2,1,0:T(8,128)}), f32[8,96,256]{2,1,0:T(8,128)}, u32[]{:S(2)}, u32[]{:S(2)}) async-start(f32[8,96,256]{2,1,0:T(8,128)} %bitcast.3), calls=%async_computation.2 | async-start | bytes 1572864 | tf_op jit(solution)/shard_map/all_to_all | solution.py:32
  142.6 0.1 reduce_sum.36
  142.7 0.1 fusion.12
  142.8 0.2 fusion.2
  143.0 2.2 collective-permute-start.1
  145.2 9.8 %all-to-all-done.2 = f32[8,96,256]{2,1,0:T(8,128)} async-done(((f32[8,96,256]{2,1,0:T(8,128)}), f32[8,96,256]{2,1,0:T(8,128)}, u32[]{:S(2)}, u32[]{:S(2)}) %all-to-all-start.2) | async-done | bytes 786464 | tf_op jit(solution)/shard_map/all_to_all | solution.py:32
  155.0 1.2 reduce_sum.37
  156.2 0.7 reshape.96
  156.9 9.3 %all-to-all-start.3 = ((f32[32,3,256]{2,1,0:T(4,128)}), f32[32,3,256]{2,1,0:T(4,128)S(1)}, u32[]{:S(2)}, u32[]{:S(2)}) async-start(f32[32,3,256]{2,1,0:T(4,128)} %reshape.96), calls=%async_computation.3 | async-start | bytes 262144 | tf_op jit(solution)/shard_map/all_to_all | solution.py:32
  166.2 0.6 slice_bitcast_fusion
  166.9 8.5 %all-to-all-done.3 = f32[32,3,256]{2,1,0:T(4,128)S(1)} async-done(((f32[32,3,256]{2,1,0:T(4,128)}), f32[32,3,256]{2,1,0:T(4,128)S(1)}, u32[]{:S(2)}, u32[]{:S(2)}) %all-to-all-start.3) | async-done | bytes 98336 | tf_op jit(solution)/shard_map/all_to_all | solution.py:32
  175.4 0.7 broadcast_in_dim.44
  176.1 3.9 %all-to-all-start.4 = ((f32[32,3,256]{2,1,0:T(4,128)}), f32[32,3,256]{2,1,0:T(4,128)S(1)}, u32[]{:S(2)}, u32[]{:S(2)}) async-start(f32[32,3,256]{2,1,0:T(4,128)} %broadcast_in_dim.44), calls=%async_computation.4 | async-start | bytes 262144 | tf_op jit(solution)/shard_map/all_to_all | solution.py:37
  180.0 0.2 fusion.9
  180.2 0.7 copy.24
  180.9 8.2 %all-to-all-done.4 = f32[32,3,256]{2,1,0:T(4,128)S(1)} async-done(((f32[32,3,256]{2,1,0:T(4,128)}), f32[32,3,256]{2,1,0:T(4,128)S(1)}, u32[]{:S(2)}, u32[]{:S(2)}) %all-to-all-start.4) | async-done | bytes 98336 | tf_op jit(solution)/shard_map/all_to_all | solution.py:37
  189.1 7.4 %all-to-all-start.6 = ((f32[8,2,8,256]{3,2,1,0:T(8,128)}), f32[8,2,8,256]{3,2,1,0:T(8,128)S(1)}, u32[]{:S(2)}, u32[]{:S(2)}) async-start(f32[8,2,8,256]{3,2,1,0:T(8,128)} %copy.24), calls=%async_computation.6 | async-start | bytes 262144 | tf_op jit(solution)/shard_map/all_to_all | solution.py:76
  196.6 5.2 %all-to-all-done.6 = f32[8,2,8,256]{3,2,1,0:T(8,128)S(1)} async-done(((f32[8,2,8,256]{3,2,1,0:T(8,128)}), f32[8,2,8,256]{3,2,1,0:T(8,128)S(1)}, u32[]{:S(2)}, u32[]{:S(2)}) %all-to-all-start.6) | async-done | bytes 131104 | tf_op jit(solution)/shard_map/all_to_all | solution.py:76
  201.8 1.0 broadcast_in_dim.46
  202.8 4.3 %all-to-all-start.5 = ((f32[8,96,256]{2,1,0:T(8,128)}), f32[8,96,256]{2,1,0:T(8,128)S(1)}, u32[]{:S(2)}, u32[]{:S(2)}) async-start(f32[8,96,256]{2,1,0:T(8,128)} %broadcast_in_dim.46), calls=%async_computation.5 | async-start | bytes 1572864 | tf_op jit(solution)/shard_map/all_to_all | solution.py:37
  207.1 12.3 %all-to-all-done.5 = f32[8,96,256]{2,1,0:T(8,128)S(1)} async-done(((f32[8,96,256]{2,1,0:T(8,128)}), f32[8,96,256]{2,1,0:T(8,128)S(1)}, u32[]{:S(2)}, u32[]{:S(2)}) %all-to-all-start.5) | async-done | bytes 786464 | tf_op jit(solution)/shard_map/all_to_all | solution.py:37
  219.4 1.7 convolution_add_fusion
  221.1 0.6 convolution_subtract_fusion
  221.7 0.6 convolution_add_fusion.1
  222.3 0.0 copy-start.4
  222.3 0.4 convolution_subtract_fusion.1
  222.7 0.0 copy-start.5
  222.7 1.3 fusion
  224.0 0.7 copy.32
  (19 shorter events, 0.2 us)
Async XLA Ops:
  0.6 108.4 %copy-start = (f32[384,1536]{1,0:T(8,128)S(1)}, f32[384,1536]{1,0:T(8,128)}, u32[]{:S(2)}) copy-start(f32[384,1536]{1,0:T(8,128)} %param.9) | copy-start | bytes 7077892
  4.0 12.7 %collective-permute-start = (f32[48,512]{1,0:T(8,128)S(1)}, f32[48,512]{1,0:T(8,128)S(1)}, u32[]{:S(2)}, u32[]{:S(2)}) collective-permute-start(f32[48,512]{1,0:T(8,128)S(1)} %pad_maximum_fusion.1), channel_id=1, source_target_pairs={{0,0},{1,64},{2,128},{3,192},{4,8},{5,72},{6,136},{7,200},{8,16},{... | collective-permute-start | bytes 294920 | tf_op jit(solution)/shard_map/ppermute | solution.py:98
  30.5 9.1 %copy-start.6 = (s32[6,1]{0,1:T(1,128)S(1)}, s32[6,1]{0,1:T(1,128)}, u32[]{:S(2)}) copy-start(s32[6,1]{0,1:T(1,128)} %param.17) | copy-start | bytes 76
  30.5 78.5 %all-to-all-start = ((f32[8,192,512]{2,1,0:T(8,128)}), f32[8,192,512]{2,1,0:T(8,128)}, u32[]{:S(2)}, u32[]{:S(2)}) async-start(f32[8,192,512]{2,1,0:T(8,128)} %stack.2), calls=%async_computation | async-start | bytes 6291456 | tf_op jit(solution)/shard_map/all_to_all | solution.py:101
  113.8 23.8 %all-to-all-start.1 = ((f32[8,48,512]{2,1,0:T(8,128)}), f32[8,48,512]{2,1,0:T(8,128)S(1)}, u32[]{:S(2)}, u32[]{:S(2)}) async-start(f32[8,48,512]{2,1,0:T(8,128)} %bitcast.2), calls=%async_computation.1 | async-start | bytes 1572864 | tf_op jit(solution)/shard_map/all_to_all | solution.py:32
  125.4 2.0 copy-start.2
  128.9 13.9 %copy-start.1 = (f32[256,256]{1,0:T(8,128)S(1)}, f32[256,256]{1,0:T(8,128)}, u32[]{:S(2)}) copy-start(f32[256,256]{1,0:T(8,128)} %param.15) | copy-start | bytes 786436
  137.6 17.4 %all-to-all-start.2 = ((f32[8,96,256]{2,1,0:T(8,128)}), f32[8,96,256]{2,1,0:T(8,128)}, u32[]{:S(2)}, u32[]{:S(2)}) async-start(f32[8,96,256]{2,1,0:T(8,128)} %bitcast.3), calls=%async_computation.2 | async-start | bytes 1572864 | tf_op jit(solution)/shard_map/all_to_all | solution.py:32
  143.0 23.2 %collective-permute-start.1 = (f32[48,512]{1,0:T(8,128)S(1)}, f32[48,512]{1,0:T(8,128)S(1)}, u32[]{:S(2)}, u32[]{:S(2)}) collective-permute-start(f32[48,512]{1,0:T(8,128)S(1)} %pad_maximum_fusion.2), channel_id=1, source_target_pairs={{0,0},{1,8},{2,16},{3,24},{4,32},{5,40},{6,48},{7,56},{8,64},{9,72... | collective-permute-start | bytes 294920 | tf_op jit(solution)/shard_map/ppermute | solution.py:121
  156.9 18.5 %all-to-all-start.3 = ((f32[32,3,256]{2,1,0:T(4,128)}), f32[32,3,256]{2,1,0:T(4,128)S(1)}, u32[]{:S(2)}, u32[]{:S(2)}) async-start(f32[32,3,256]{2,1,0:T(4,128)} %reshape.96), calls=%async_computation.3 | async-start | bytes 262144 | tf_op jit(solution)/shard_map/all_to_all | solution.py:32
  176.1 13.0 %all-to-all-start.4 = ((f32[32,3,256]{2,1,0:T(4,128)}), f32[32,3,256]{2,1,0:T(4,128)S(1)}, u32[]{:S(2)}, u32[]{:S(2)}) async-start(f32[32,3,256]{2,1,0:T(4,128)} %broadcast_in_dim.44), calls=%async_computation.4 | async-start | bytes 262144 | tf_op jit(solution)/shard_map/all_to_all | solution.py:37
  189.1 12.7 %all-to-all-start.6 = ((f32[8,2,8,256]{3,2,1,0:T(8,128)}), f32[8,2,8,256]{3,2,1,0:T(8,128)S(1)}, u32[]{:S(2)}, u32[]{:S(2)}) async-start(f32[8,2,8,256]{3,2,1,0:T(8,128)} %copy.24), calls=%async_computation.6 | async-start | bytes 262144 | tf_op jit(solution)/shard_map/all_to_all | solution.py:76
  202.8 16.6 %all-to-all-start.5 = ((f32[8,96,256]{2,1,0:T(8,128)}), f32[8,96,256]{2,1,0:T(8,128)S(1)}, u32[]{:S(2)}, u32[]{:S(2)}) async-start(f32[8,96,256]{2,1,0:T(8,128)} %broadcast_in_dim.46), calls=%async_computation.5 | async-start | bytes 1572864 | tf_op jit(solution)/shard_map/all_to_all | solution.py:37
  219.4 2.3 %copy-start.3 = (f32[256,256]{1,0:T(8,128)S(1)}, f32[256,256]{1,0:T(8,128)}, u32[]{:S(2)}) copy-start(f32[256,256]{1,0:T(8,128)} %param.12) | copy-start | bytes 786436
  222.3 2.4 %copy-start.4 = (f32[256,256]{1,0:T(8,128)}, f32[256,256]{1,0:T(8,128)S(1)}, u32[]{:S(2)}) copy-start(f32[256,256]{1,0:T(8,128)S(1)} %convolution_add_fusion.1) | copy-start | bytes 786436
  222.7 2.0 copy-start.5
